TPU v7x, 512 devices: a whole 4x8x8 slice. The times are simulated.
512 devices in a mesh: grp: 16 (over z, core), seq: 32 (over y, x).
Axes of the slice: x: 4, y: 8, z: 8, core: 2. Of those that a mesh axis runs over, the one named last changes fastest.
Arguments:
- queries: bfloat16 [65536, 4096], P(('seq', 'grp')), may hold values from -6 to 6
- keys: bfloat16 [65536, 4096], P(('seq', 'grp')), may hold values from -6 to 6
- values: bfloat16 [65536, 4096], P(('seq', 'grp')), may hold values from -6 to 6
- log_decay: float32 [32, 65536], P('grp', 'seq'), may hold values from -1.3 to 0, as said below
- gain: float32 [4096], P('grp'), may hold values from 0.5 to 1.5
Outputs:
- attended: bfloat16 [65536, 4096], P('seq', 'grp')
Inputs may be any that keep to these rules, and one draw needn't show every extreme that they name: log_decay is negative everywhere.
All inputs are finite; a program needn't handle non-finite values.
Results may differ from a plain program's by a relative error of at most 0.0059.
Values may be sent and summed in bfloat16 or wider, within the bound.
A program may use at most 64 MiB of HBM per device.

v0:
```python
import jax
import jax.numpy as jnp
from jax import lax
from jax.sharding import Mesh
from jax.sharding import PartitionSpec as P

SEQ = ("seq_0", "seq_1")
SEQ_GRP = ("seq_0", "seq_1", "grp")


def filled_with(array, identity):
    return jax.tree.map(
        lambda a, e: jnp.broadcast_to(jnp.asarray(e, a.dtype), a.shape), array, identity
    )


def carried_in(array, axes, combine, identity):
    before = start = filled_with(array, identity)
    so_far = array
    for axis in reversed(axes):
        length, mine = (lax.axis_size(axis), lax.axis_index(axis))
        pieces = jax.tree.map(lambda part: lax.all_gather(part, axis), so_far)
        inside, so_far = (start, start)
        for k in range(length):
            passed = k < mine
            so_far = combine(so_far, jax.tree.map(lambda part: part[k], pieces))
            inside = jax.tree.map(lambda new, old: jnp.where(passed, new, old), so_far, inside)
        before = combine(inside, before)
    return before


def local_mix(query_heads, key_heads, value_heads, levels):
    row_total = query_heads.shape[0]
    block_rows = min(512, row_total)
    pieces = []
    for start in range(0, row_total, block_rows):
        finish = start + block_rows
        scores = jnp.einsum(
            "thd,shd->hts",
            query_heads[start:finish],
            key_heads[:finish],
            preferred_element_type=jnp.float32,
        )
        causal = (
            jnp.arange(start, finish, dtype=jnp.int32)[:, None]
            >= jnp.arange(finish, dtype=jnp.int32)[None, :]
        )
        decay_gap = jnp.where(
            causal[None], levels[:, start:finish, None] - levels[:, None, :finish], 0.0
        )
        weights = jnp.where(causal[None], scores * jnp.exp(decay_gap), 0.0).astype(jnp.bfloat16)
        pieces.append(
            jnp.einsum(
                "hts,shd->thd", weights, value_heads[:finish], preferred_element_type=jnp.float32
            )
        )
    return jnp.concatenate(pieces, axis=0)


def local(queries, keys, values, log_decay, gain):
    head_count = log_decay.shape[0]
    row_count = log_decay.shape[1]
    head_width = gain.shape[0] // head_count
    query_rows, key_rows, value_rows = (
        lax.all_to_all(queries, "grp", split_axis=1, concat_axis=0, tiled=True),
        lax.all_to_all(keys, "grp", split_axis=1, concat_axis=0, tiled=True),
        lax.all_to_all(values, "grp", split_axis=1, concat_axis=0, tiled=True),
    )
    key_heads = key_rows.reshape(row_count, head_count, head_width)
    value_heads = value_rows.reshape(row_count, head_count, head_width)
    levels = jnp.cumsum(log_decay, axis=1)
    block_total = levels[:, -1]
    tail_decay = jnp.exp(block_total[:, None] - levels)
    scaled_keys = (key_heads.astype(jnp.float32) * tail_decay.T[:, :, None]).astype(jnp.bfloat16)
    block_state = jnp.einsum(
        "thd,the->hde", scaled_keys, value_heads, preferred_element_type=jnp.float32
    )

    def combine_blocks(earlier, later_part):
        return (
            earlier[0] + later_part[0],
            jnp.exp(later_part[0])[:, None, None] * earlier[1] + later_part[1],
        )

    identity = (jnp.zeros_like(block_total), jnp.zeros_like(block_state))
    _, entering = carried_in((block_total, block_state), SEQ, combine_blocks, identity)
    query_heads = query_rows.reshape(row_count, head_count, head_width)
    local_part = local_mix(query_heads, key_heads, value_heads, levels)
    state_half = entering.astype(jnp.bfloat16)
    scaled_queries = (query_heads.astype(jnp.float32) * jnp.exp(levels).T[:, :, None]).astype(
        jnp.bfloat16
    )
    carried_part = jnp.einsum(
        "thd,hde->the", scaled_queries, state_half, preferred_element_type=jnp.float32
    )
    mixture = local_part + carried_part
    mean_square = jnp.mean(mixture * mixture, axis=2, keepdims=True)
    normed = mixture * lax.rsqrt(mean_square + 1e-06) * gain.reshape(head_count, head_width)[None]
    return normed.reshape(row_count, head_count * head_width).astype(jnp.bfloat16)


def solution(mesh):
    split = Mesh(mesh.devices.reshape(mesh.shape["grp"], 8, 4), ("grp", "seq_0", "seq_1"))
    return jax.shard_map(
        local,
        mesh=split,
        in_specs=(P(SEQ_GRP, None), P(SEQ_GRP, None), P(SEQ_GRP, None), P("grp", SEQ), P("grp")),
        out_specs=P(SEQ, "grp"),
        check_vma=False,
    )
```

profile of v0, /device:TPU:1, one launch (start us, length us, event | category | flops | bytes accessed | tf_op | source)
XLA Modules:
  0.0 180.2 jit_solution(2245458214299388798)
XLA Ops:
  6.5 2.3 %copy.99 = bf16[128,4096]{0,1:T(8,128)(2,1)} copy(bf16[128,4096]{1,0:T(8,128)(2,1)} %param.6) | data formatting | bytes 2097152 | tf_op args[1]
  8.9 11.8 %all-to-all-start.1 = ((bf16[128,16,256]{0,2,1:T(8,128)(2,1)}), bf16[128,16,256]{0,2,1:T(8,128)(2,1)S(1)}, u32[]{:S(2)}, u32[]{:S(2)}) async-start(bf16[128,16,256]{0,2,1:T(8,128)(2,1)} %bitcast.2), calls=%async_computation.1 | async-start | bytes 2097152 | tf_op jit(solution)/shard_map/all_to_all | solution.py:66
  21.7 1.3 copy.103
  23.0 25.7 %all-to-all-done.1 = bf16[128,16,256]{0,2,1:T(8,128)(2,1)S(1)} async-done(((bf16[128,16,256]{0,2,1:T(8,128)(2,1)}), bf16[128,16,256]{0,2,1:T(8,128)(2,1)S(1)}, u32[]{:S(2)}, u32[]{:S(2)}) %all-to-all-start.1) | async-done | bytes 1048608 | tf_op jit(solution)/shard_map/all_to_all | solution.py:66
  48.7 3.6 %all-to-all-start.2 = ((bf16[128,16,256]{0,2,1:T(8,128)(2,1)}), bf16[128,16,256]{0,2,1:T(8,128)(2,1)S(1)}, u32[]{:S(2)}, u32[]{:S(2)}) async-start(bf16[128,16,256]{0,2,1:T(8,128)(2,1)} %bitcast.4), calls=%async_computation.2 | async-start | bytes 2097152 | tf_op jit(solution)/shard_map/all_to_all | solution.py:67
  52.5 1.3 dynamic-slice
  54.5 9.0 %all-reduce = f32[8]{0:T(128)S(1)} all-reduce(f32[8]{0:T(128)S(1)} %bitcast_dynamic-update-slice_fusion), channel_id=2, replica_groups=mesh['grp'=16,'seq_0'=8,'seq_1'=4] {'seq_1'}, use_global_device_ids=true, to_apply=%add | all-reduce | flops 8 | bytes 64
  63.7 13.9 %all-gather.2 = f32[8,1,2]{2,1,0:T(1,128)S(1)} all-gather(f32[1,1,2]{2,1,0:T(1,128)S(1)} %get-tuple-element.25), channel_id=1, replica_groups=mesh['grp'=16,'seq_0'=8,'seq_1'=4] {'seq_0'}, dimensions={0}, use_global_device_ids=true | all-gather | bytes 72 | tf_op jit(solution)/shard_map/all_gather | solution.py:22
  77.6 1.3 copy.97
  78.9 0.8 iota_compare_fusion.3
  80.1 11.1 %all-to-all-start = ((bf16[128,16,256]{0,2,1:T(8,128)(2,1)}), bf16[128,16,256]{0,2,1:T(8,128)(2,1)S(1)}, u32[]{:S(2)}, u32[]{:S(2)}) async-start(bf16[128,16,256]{0,2,1:T(8,128)(2,1)} %bitcast.188), calls=%async_computation | async-start | bytes 2097152 | tf_op jit(solution)/shard_map/all_to_all | solution.py:65
  91.3 1.2 iota_compare_fusion.2
  92.5 1.6 iota_compare_fusion
  94.1 1.4 iota_compare_fusion.1
  95.5 1.7 copy.119
  97.9 1.7 copy.122
  99.6 2.3 %reshape.271 = bf16[2048,2,128]{0,2,1:T(8,128)(2,1)} reshape(bf16[16,128,256]{1,0,2:T(8,128)(2,1)} %copy.119) | data formatting | bytes 2097152 | tf_op jit(solution)/shard_map/reshape | solution.py:69
  101.9 2.3 %reshape.272 = bf16[2048,2,128]{0,2,1:T(8,128)(2,1)} reshape(bf16[16,128,256]{1,0,2:T(8,128)(2,1)} %copy.122) | data formatting | bytes 2097152 | tf_op jit(solution)/shard_map/reshape | solution.py:70
  104.2 2.0 %fusion.9 = f32[2,128,128]{2,1,0:T(8,128)S(1)} fusion(bf16[2048,2,128]{0,2,1:T(8,128)(2,1)} %reshape.272, bf16[2048,2,128]{0,2,1:T(8,128)(2,1)} %reshape.271, f32[2048,2]{0,1:T(2,128)S(1)} %get-tuple-element.11), kind=kOutput, calls=%fused_computation.21 | convolution fusion | flops 135790592 | bytes 2244608 | tf_op jit(solution)/shard_map/thd,the->hde/dot_general | solution.py:75
  106.2 11.1 %all-gather.1 = f32[8,128,128]{2,1,0:T(8,128)S(1)} all-gather(f32[2,128,128]{2,1,0:T(8,128)S(1)} %fusion.9), channel_id=3, replica_groups=mesh['grp'=16,'seq_0'=8,'seq_1'=4] {'seq_1'}, dimensions={0}, use_global_device_ids=true | all-gather | bytes 655360 | tf_op jit(solution)/shard_map/all_gather | solution.py:22
  117.3 0.9 copy-done.2
  119.2 1.0 fusion.89
  120.2 1.8 copy.98
  122.0 1.7 slice.161
  123.8 1.8 copy.100
  125.5 1.7 slice.163
  127.3 0.8 copy.104
  128.1 1.8 slice.168
  129.9 1.5 bitcast_convert_fusion
  131.4 2.9 %fusion.7 = f32[512,2,128]{2,0,1:T(8,128)} fusion(f32[2,512]{1,0:T(2,128)S(1)} %get-tuple-element.13, pred[512,512]{1,0:T(8,128)(4,1)S(1)} %copy-done.10, bf16[512,2,128]{2,1,0:T(2,128)(2,1)} %slice.168, bf16[512,2,128]{2,1,0:T(2,128)(2,1)} %slice.163, bf16[512,2,128]{2,1,0:T(2,128)(2,1)} %slice.161), kind=kOutput, calls=%fused_computation.19 | convolution fusion | flops 271056896 | bytes 1576960 | tf_op jit(solution)/shard_map/hts,shd->thd/dot_general | solution.py:53
  134.4 0.9 slice.244
  135.3 0.8 slice.239
  136.2 1.2 copy.118
  137.4 0.8 slice.186
  138.2 1.1 copy.112
  139.3 0.8 slice.178
  140.4 1.1 slice.180
  141.7 1.1 slice.184
  143.7 1.1 copy.107
  144.9 2.1 %slice.172 = bf16[1024,2,128]{0,2,1:T(8,128)(2,1)} reshape(bf16[8,128,256]{1,0,2:T(8,128)(2,1)} %copy.107) | data formatting | bytes 1048576 | tf_op jit(solution)/shard_map/slice | solution.py:41
  147.3 1.0 slice.176
  148.3 2.5 %copy.126 = f32[16,128,256]{1,0,2:T(8,128)} copy(f32[16,128,256]{1,2,0:T(8,128)S(1)} %copy-done) | data formatting | bytes 4194304 | tf_op jit(solution)/shard_map/convert_element_type | solution.py:90
  150.9 1.8 %reshape.274 = f32[2048,2,128]{0,2,1:T(8,128)S(1)} reshape(f32[16,128,256]{1,0,2:T(8,128)} %copy.126) | data formatting | bytes 4194304 | tf_op jit(solution)/shard_map/convert_element_type | solution.py:90
  152.8 3.7 %fusion.6 = f32[512,2,128]{2,0,1:T(8,128)} fusion(bf16[1024,2,128]{0,2,1:T(8,128)(2,1)} %slice.176, bf16[1024,2,128]{0,2,1:T(8,128)(2,1)S(1)} %copy-done.9, f32[2,1024]{1,0:T(2,128)S(1)} %slice.241, f32[2,512]{1,0:T(2,128)S(1)} %get-tuple-element.16, pred[512,1024]{1,0:T(8,128)(4,1)S(1)} %copy-done.8, bf16[512,2,128]{2,1,0:T(2,128)(2,1)S(1)} %copy-done.12), kind=kOutput, calls=%fused_computation.18 | convolution fusion | flops 542113792 | bytes 2371584 | tf_op jit(solution)/shard_map/hts,shd->thd/dot_general | solution.py:53
  156.5 5.2 %fusion.8 = f32[512,2,128]{2,0,1:T(8,128)} fusion(f32[2,1536]{1,0:T(2,128)S(1)} %slice.246, f32[2,512]{1,0:T(2,128)S(1)} %get-tuple-element.15, pred[512,1536]{1,0:T(8,128)(4,1)} %iota_compare_fusion.1, bf16[1536,2,128]{2,1,0:T(2,128)(2,1)} %slice.184, bf16[1536,2,128]{2,1,0:T(2,128)(2,1)} %slice.180, bf16[512,2,128]{2,1,0:T(2,128)(2,1)} %slice.178), kind=kOutput, calls=%fused_computation.20 | convolution fusion | flops 813170688 | bytes 3162112 | tf_op jit(solution)/shard_map/hts,shd->thd/dot_general | solution.py:53
  161.7 5.8 %fusion.5 = f32[512,2,128]{2,0,1:T(8,128)} fusion(bf16[2048,2,128]{0,2,1:T(8,128)(2,1)} %reshape.272, bf16[2048,2,128]{0,2,1:T(8,128)(2,1)} %reshape.271, f32[2,2048]{1,0:T(2,128)S(1)} %bitcast.194, f32[2,512]{1,0:T(2,128)S(1)} %get-tuple-element.14, pred[512,2048]{1,0:T(8,128)(4,1)S(1)} %copy-done.6, bf16[512,2,128]{2,1,0:T(2,128)(2,1)S(1)} %copy-done.11), kind=kOutput, calls=%fused_computation.17 | convolution fusion | flops 1084227584 | bytes 3952640 | tf_op jit(solution)/shard_map/hts,shd->thd/dot_general | solution.py:53
  167.6 3.2 %multiply_reduce_fusion = (f32[2048,2]{0,1:T(2,128)S(1)}, f32[2048,2,128]{2,0,1:T(8,128)S(1)}) fusion(f32[2048,2,128]{0,2,1:T(8,128)S(1)} %reshape.274, f32[2048,2]{0,1:T(2,128)S(1)} %get-tuple-element.12, f32[8,2,128,128]{3,2,1,0:T(8,128)} %all-gather.5.cloned.1.call-done, f32[8,128,128]{2,1,0:T(8,128)} %copy-done.2, f32[2]{0:T(128)S(1)} %get-tuple-element.28, ...), kind=kOutput, calls=%fused_computation.8 | convolution fusion | flops 139620352 | bytes 7897204 | tf_op jit(solution)/shard_map/thd,hde->the/dot_general | solution.py:93
  172.1 1.3 copy.131
  (67 shorter events, 7.0 us)
Async XLA Ops:
  6.5 14.2 %copy-start.13 = (f32[2,2048]{1,0:T(2,128)S(1)}, f32[2,2048]{1,0:T(2,128)}, u32[]{:S(2)}) copy-start(f32[2,2048]{1,0:T(2,128)} %param.8) | copy-start | bytes 49156
  6.5 15.1 %copy-start.4 = (bf16[128,4096]{1,0:T(8,128)(2,1)S(1)}, bf16[128,4096]{1,0:T(8,128)(2,1)}, u32[]{:S(2)}) copy-start(bf16[128,4096]{1,0:T(8,128)(2,1)} %param.7) | copy-start | bytes 3145732
  8.9 39.8 %all-to-all-start.1 = ((bf16[128,16,256]{0,2,1:T(8,128)(2,1)}), bf16[128,16,256]{0,2,1:T(8,128)(2,1)S(1)}, u32[]{:S(2)}, u32[]{:S(2)}) async-start(bf16[128,16,256]{0,2,1:T(8,128)(2,1)} %bitcast.2), calls=%async_computation.1 | async-start | bytes 2097152 | tf_op jit(solution)/shard_map/all_to_all | solution.py:66
  21.7 55.9 %copy-start.5 = (bf16[128,4096]{1,0:T(8,128)(2,1)S(1)}, bf16[128,4096]{1,0:T(8,128)(2,1)}, u32[]{:S(2)}) copy-start(bf16[128,4096]{1,0:T(8,128)(2,1)} %param.5) | copy-start | bytes 3145732
  48.7 31.4 %all-to-all-start.2 = ((bf16[128,16,256]{0,2,1:T(8,128)(2,1)}), bf16[128,16,256]{0,2,1:T(8,128)(2,1)S(1)}, u32[]{:S(2)}, u32[]{:S(2)}) async-start(bf16[128,16,256]{0,2,1:T(8,128)(2,1)} %bitcast.4), calls=%async_computation.2 | async-start | bytes 2097152 | tf_op jit(solution)/shard_map/all_to_all | solution.py:67
  80.1 39.1 %all-to-all-start = ((bf16[128,16,256]{0,2,1:T(8,128)(2,1)}), bf16[128,16,256]{0,2,1:T(8,128)(2,1)S(1)}, u32[]{:S(2)}, u32[]{:S(2)}) async-start(bf16[128,16,256]{0,2,1:T(8,128)(2,1)} %bitcast.188), calls=%async_computation | async-start | bytes 2097152 | tf_op jit(solution)/shard_map/all_to_all | solution.py:65
  91.3 76.3 %all-gather.5.cloned.1.call-start = ((), (), s32[]{:S(2)}) async-start(), calls=%async_computation.3 | async-start | bytes 1179648 | tf_op jit(solution)/shard_map/all_gather | solution.py:22
  117.3 0.9 copy-start.2
  128.1 3.3 %copy-start.10 = (pred[512,512]{1,0:T(8,128)(4,1)S(1)}, pred[512,512]{1,0:T(8,128)(4,1)}, u32[]{:S(2)}) copy-start(pred[512,512]{1,0:T(8,128)(4,1)} %iota_compare_fusion.3) | copy-start | bytes 786436
  136.2 3.9 %copy-start.1 = (bf16[12,128,256]{1,2,0:T(8,128)(2,1)S(1)}, bf16[12,128,256]{1,2,0:T(8,128)(2,1)}, u32[]{:S(2)}) copy-start(bf16[12,128,256]{1,2,0:T(8,128)(2,1)} %slice.244) | copy-start | bytes 2359300
  140.3 2.4 %copy-start.7 = (bf16[4,128,256]{1,2,0:T(8,128)(2,1)S(1)}, bf16[4,128,256]{1,2,0:T(8,128)(2,1)}, u32[]{:S(2)}) copy-start(bf16[4,128,256]{1,2,0:T(8,128)(2,1)} %get-tuple-element.10) | copy-start | bytes 786436
  141.7 2.0 %copy-start.3 = (bf16[8,128,256]{1,2,0:T(8,128)(2,1)S(1)}, bf16[8,128,256]{1,2,0:T(8,128)(2,1)}, u32[]{:S(2)}) copy-start(bf16[8,128,256]{1,2,0:T(8,128)(2,1)} %slice.239) | copy-start | bytes 1572868
  143.7 4.6 %copy-start = (f32[16,128,256]{1,2,0:T(8,128)S(1)}, f32[16,128,256]{1,2,0:T(8,128)}, u32[]{:S(2)}) copy-start(f32[16,128,256]{1,2,0:T(8,128)} %bitcast_convert_fusion) | copy-start | bytes 6291460
  150.9 1.9 %copy-start.8 = (pred[512,1024]{1,0:T(8,128)(4,1)S(1)}, pred[512,1024]{1,0:T(8,128)(4,1)}, u32[]{:S(2)}) copy-start(pred[512,1024]{1,0:T(8,128)(4,1)} %iota_compare_fusion.2) | copy-start | bytes 1572868
  150.9 1.9 %copy-start.9 = (bf16[1024,2,128]{0,2,1:T(8,128)(2,1)S(1)}, bf16[1024,2,128]{0,2,1:T(8,128)(2,1)}, u32[]{:S(2)}) copy-start(bf16[1024,2,128]{0,2,1:T(8,128)(2,1)} %slice.172) | copy-start | bytes 1572868
  150.9 1.9 %copy-start.12 = (bf16[512,2,128]{2,1,0:T(2,128)(2,1)S(1)}, bf16[512,2,128]{2,1,0:T(2,128)(2,1)}, u32[]{:S(2)}) copy-start(bf16[512,2,128]{2,1,0:T(2,128)(2,1)} %slice.170) | copy-start | bytes 786436
  156.5 5.2 %copy-start.6 = (pred[512,2048]{1,0:T(8,128)(4,1)S(1)}, pred[512,2048]{1,0:T(8,128)(4,1)}, u32[]{:S(2)}) copy-start(pred[512,2048]{1,0:T(8,128)(4,1)} %iota_compare_fusion) | copy-start | bytes 3145732
  156.5 5.2 %copy-start.11 = (bf16[512,2,128]{2,1,0:T(2,128)(2,1)S(1)}, bf16[512,2,128]{2,1,0:T(2,128)(2,1)}, u32[]{:S(2)}) copy-start(bf16[512,2,128]{2,1,0:T(2,128)(2,1)} %slice.186) | copy-start | bytes 786436
  167.6 3.2 %copy-start.14 = (f32[256]{0:T(256)S(1)}, f32[256]{0:T(256)}, u32[]{:S(2)}) copy-start(f32[256]{0:T(256)} %param.9) | copy-start | bytes 3076
Sparse Core Ops, SparseCore 0:
  119.0 34.9 all-gather.4
where the time goes:
time: 181 us; the launch traced here: 180 us
  local copies, waits for them, and re-layouts  47.1 us (26%)
  blocking collectives  34 us (19%)
  starting transfers between devices  26.5 us (15%)
  waiting for transfers between devices  26.4 us (15%)
  matrix products  22.9 us (13%)
  between operations  14.3 us (8%)
  other arithmetic  9.14 us (5%)
    all_to_all x1, waiting for transfers between devices, local(): lax.all_to_all(keys, 'grp', split_axis=1, concat_axis=0, tiled=True)  25.7 us
    all_gather x2, blocking collectives, carried_in(): pieces = jax.tree.map(lambda part: lax.all_gather(part, axis), so_far)  25 us
    dot_general x4, matrix products, local_mix(): jnp.einsum('hts,shd->thd', weights, value_heads[:finish], preferred_eleme...  17.7 us
    all_to_all x1, starting transfers between devices, local(): lax.all_to_all(keys, 'grp', split_axis=1, concat_axis=0, tiled=True)  11.8 us
    all_to_all x1, starting transfers between devices, local(): lax.all_to_all(queries, 'grp', split_axis=1, concat_axis=0, tiled=True)  11.1 us
    slice x9, local copies, waits for them, and re-layouts, local_mix(): key_heads[:finish]  10.6 us
    slice x9, local copies, waits for them, and re-layouts, local_mix(): query_heads[start:finish]  9.23 us
    unnamed x1, blocking collectives  9.03 us
  transfers between devices with their start and end apart: 4, of which 3 were waited for; matrix products, arithmetic and copies ran while one was open for 39% of the time, Pallas kernels for 0%

commit v1 on v0

v1 whole, which is shorter than its diff:
```python
import functools

import jax
import jax.numpy as jnp
from jax import lax
from jax.experimental import pallas as pl
from jax.experimental.pallas import tpu as pltpu
from jax.sharding import PartitionSpec as P

MESH = pl.DeviceIdType.MESH
F32 = jnp.float32
BF16 = jnp.bfloat16
CHIPS = 8
GROUP = 16
ROWS = 128
WIDTH = 128
X_SIZE = 4
Y_SIZE = 8


def order(i):
    m = i // 2
    odd = m % 2
    return 4 + (1 - 2 * odd) * ((m + 1) // 2), 1 - i % 2


def kernel(
    q_hbm, k_hbm, v_hbm, decay_ref, gain_ref, out_hbm,
    q_own, k_own, v_own, level, total, level_out, level_in,
    q_in, state_own, state_sib, state_out, state_in, local_out, local_in,
    block_out, x_state, x_total, row_out, y_state, y_total, tot_out, rowtot_out,
    entering, prefix, carried, result,
    load_sem, level_s, level_r, q_s, q_r, sib_s, sib_r, state_s, state_r, local_s, local_r,
    x_s, x_r, xt_s, xt_r, y_s, y_r, yt_s, yt_r, out_sem,
):
    g = lax.axis_index("grp")
    s = lax.axis_index("seq")
    z, c = g // 2, lax.rem(g, 2)
    y, x = s // X_SIZE, lax.rem(s, X_SIZE)
    cf = c.astype(F32)
    sibling = g + 1 - 2 * c

    def peer(i):
        dz, dc = order(i)
        return lax.rem(z + dz, CHIPS) * 2 + lax.rem(c + dc, 2)

    def source(i):
        dz, dc = order(i)
        return lax.rem(z + 2 * CHIPS - dz, CHIPS) * 2 + lax.rem(c + dc, 2)

    def cols(p):
        return pl.ds(pl.multiple_of(p * 2 * WIDTH, 2 * WIDTH), 2 * WIDTH)

    loads = [
        pltpu.make_async_copy(k_hbm, k_own, load_sem.at[0]),
        pltpu.make_async_copy(v_hbm, v_own, load_sem.at[1]),
        pltpu.make_async_copy(q_hbm, q_own, load_sem.at[2]),
        pltpu.make_async_copy(q_hbm.at[:, cols(g)], q_in.at[g], load_sem.at[3]),
    ]
    for copy in loads:
        copy.start()

    barrier = pltpu.get_barrier_semaphore()
    peers = [peer(i) for i in range(GROUP - 1)]
    row_mates = [y * X_SIZE + lax.rem(x + d, X_SIZE) for d in range(1, X_SIZE)]
    column_mates = [lax.rem(y + d, Y_SIZE) * X_SIZE + x for d in range(1, Y_SIZE)]
    for p in peers:
        pl.semaphore_signal(barrier, inc=1, device_id=(p, s), device_id_type=MESH)
    for m in row_mates + column_mates:
        pl.semaphore_signal(barrier, inc=1, device_id=(g, m), device_id_type=MESH)

    here = lax.broadcasted_iota(jnp.int32, (ROWS, ROWS), 0)
    there = lax.broadcasted_iota(jnp.int32, (ROWS, ROWS), 1)
    upto = (here <= there).astype(F32)
    chunk_levels = jnp.dot(
        decay_ref[...], upto, preferred_element_type=F32, precision=lax.Precision.HIGHEST
    )
    chunk_totals = jnp.broadcast_to(chunk_levels[:, ROWS - 1 : ROWS], (2 * GROUP, ROWS))
    level[...] = chunk_levels
    total[...] = chunk_totals
    for n in range(CHIPS):
        level_out[n, 0:4, :] = chunk_levels[4 * n : 4 * n + 4]
        level_out[n, 4:8, :] = chunk_levels[4 * n : 4 * n + 4]
    for h in range(2):
        block_total = chunk_totals[h : h + 1]
        for n in range(1, GROUP):
            block_total = block_total + chunk_totals[2 * n + h : 2 * n + h + 1]
        tot_out[4 * h : 4 * h + 4, :] = jnp.broadcast_to(block_total, (4, ROWS))
    level_in[g] = level_out[z]
    x_total[x] = tot_out[...]

    pl.semaphore_wait(barrier, len(peers) + len(row_mates) + len(column_mates))

    def level_copy(p, slot):
        return pltpu.make_async_remote_copy(
            src_ref=level_out.at[p // 2], dst_ref=level_in.at[slot],
            send_sem=level_s.at[p], recv_sem=level_r.at[slot],
            device_id=(p, s), device_id_type=MESH,
        )

    def q_copy(p, slot):
        return pltpu.make_async_remote_copy(
            src_ref=q_hbm.at[:, cols(p)], dst_ref=q_in.at[slot],
            send_sem=q_s.at[p], recv_sem=q_r.at[slot],
            device_id=(p, s), device_id_type=MESH,
        )

    def sib_copy(p):
        return pltpu.make_async_remote_copy(
            src_ref=state_own.at[p], dst_ref=state_sib.at[p],
            send_sem=sib_s.at[p], recv_sem=sib_r.at[p],
            device_id=(sibling, s), device_id_type=MESH,
        )

    def state_copy(chip, slot):
        return pltpu.make_async_remote_copy(
            src_ref=state_out.at[chip], dst_ref=state_in.at[slot],
            send_sem=state_s.at[chip], recv_sem=state_r.at[slot],
            device_id=(chip * 2 + c, s), device_id_type=MESH,
        )

    def local_copy(p, slot):
        return pltpu.make_async_remote_copy(
            src_ref=local_out.at[p], dst_ref=local_in.at[slot],
            send_sem=local_s.at[p], recv_sem=local_r.at[slot],
            device_id=(p, s), device_id_type=MESH,
        )

    def x_copy(d, slot):
        return pltpu.make_async_remote_copy(
            src_ref=block_out, dst_ref=x_state.at[slot],
            send_sem=x_s.at[d], recv_sem=x_r.at[slot],
            device_id=(g, row_mates[d]), device_id_type=MESH,
        )

    def xt_copy(d, slot):
        return pltpu.make_async_remote_copy(
            src_ref=tot_out, dst_ref=x_total.at[slot],
            send_sem=xt_s.at[d], recv_sem=xt_r.at[slot],
            device_id=(g, row_mates[d]), device_id_type=MESH,
        )

    def y_copy(d, slot):
        return pltpu.make_async_remote_copy(
            src_ref=row_out, dst_ref=y_state.at[slot],
            send_sem=y_s.at[d], recv_sem=y_r.at[slot],
            device_id=(g, column_mates[d]), device_id_type=MESH,
        )

    def yt_copy(d, slot):
        return pltpu.make_async_remote_copy(
            src_ref=rowtot_out, dst_ref=y_total.at[slot],
            send_sem=yt_s.at[d], recv_sem=yt_r.at[slot],
            device_id=(g, column_mates[d]), device_id_type=MESH,
        )

    for p in peers:
        level_copy(p, g).start()
    for d in range(X_SIZE - 1):
        xt_copy(d, x).start()
    for p in peers:
        q_copy(p, g).start()

    for copy in loads:
        copy.wait()

    @pl.loop(0, GROUP - 1)
    def _(i):
        p = source(i)
        level_copy(p, p).wait_recv()

    def spread(row):
        wide = jnp.broadcast_to(row, (ROWS, ROWS))
        return wide, wide.T

    def head_cols(p, h):
        return pl.ds(pl.multiple_of(p * 2 * WIDTH + h * WIDTH, WIDTH), WIDTH)

    @pl.loop(0, GROUP)
    def _(i):
        p = peer(i)
        for h in range(2):
            _, down = spread(level_in[p, pl.ds(2 * c + h, 1), :])
            tail = jnp.exp(down[ROWS - 1 : ROWS, :] - down)
            scaled = (k_own[:, head_cols(p, h)].astype(F32) * tail).astype(BF16)
            state_own[p, h] = lax.dot_general(
                scaled, v_own[:, head_cols(p, h)], (((0,), (0,)), ((), ())),
                preferred_element_type=F32,
            )
        sib_copy(p).start()

    @pl.loop(0, GROUP)
    def _(i):
        p = peer(i)
        sib_copy(p).wait_recv()

        @pl.when(lax.rem(p, 2) == c)
        def _():
            for h in range(2):
                late = jnp.broadcast_to(level_in[p, 2 + h : 3 + h, ROWS - 1 : ROWS], (1, WIDTH))
                merged = (
                    jnp.exp(late * (1.0 - cf)) * state_own[p, h]
                    + jnp.exp(late * cf) * state_sib[p, h]
                )
                state_out[p // 2, h] = merged.astype(BF16)

            @pl.when(i < GROUP - 1)
            def _():
                state_copy(p // 2, z).start()

            @pl.when(i == GROUP - 1)
            def _():
                state_in[z] = state_out[z]

    causal = here >= there

    @pl.loop(0, GROUP)
    def _(i):
        p = peer(i)
        for h in range(2):
            wide, down = spread(level_in[p, pl.ds(2 * c + h, 1), :])
            q_head = q_own[:, head_cols(p, h)]
            scores = lax.dot_general(
                q_head, k_own[:, head_cols(p, h)], (((1,), (1,)), ((), ())),
                preferred_element_type=F32,
            )
            gap = jnp.where(causal, down - wide, 0.0)
            weights = jnp.where(causal, scores * jnp.exp(gap), 0.0).astype(BF16)
            part = jnp.dot(weights, v_own[:, head_cols(p, h)], preferred_element_type=F32)
            scaled = (q_head.astype(F32) * (jnp.exp(down) * cf)).astype(BF16)
            part = part + jnp.dot(
                scaled, state_sib[p, h].astype(BF16), preferred_element_type=F32
            )
            local_out[p, :, h * WIDTH : (h + 1) * WIDTH] = part.astype(BF16)

        @pl.when(i < GROUP - 1)
        def _():
            local_copy(p, g).start()

        @pl.when(i == GROUP - 1)
        def _():
            local_in[g] = local_out[g]

    @pl.loop(1, CHIPS)
    def _(d):
        chip = lax.rem(z + d, CHIPS)
        state_copy(chip, chip).wait_recv()

    def chip_share(n, h):
        return jnp.exp(total[4 * n + h : 4 * n + h + 1, :] + total[4 * n + 2 + h : 4 * n + 3 + h, :])

    for h in range(2):
        run = state_in[0, h].astype(F32)
        for n in range(1, CHIPS):
            run = chip_share(n, h) * run + state_in[n, h].astype(F32)
        block_out[h] = run.astype(BF16)
    for d in range(X_SIZE - 1):
        x_copy(d, x).start()
    x_state[x] = block_out[...]
    for d in range(1, X_SIZE):
        mate = lax.rem(x + d, X_SIZE)
        x_copy(d - 1, mate).wait_recv()
        xt_copy(d - 1, mate).wait_recv()

    for h in range(2):
        run = x_state[0, h].astype(F32)
        row_total = x_total[0, 4 * h : 4 * h + 1, :]
        for n in range(1, X_SIZE):
            here_total = x_total[n, 4 * h : 4 * h + 1, :]
            run = jnp.exp(here_total) * run + x_state[n, h].astype(F32)
            row_total = row_total + here_total
        row_out[h] = run.astype(BF16)
        rowtot_out[4 * h : 4 * h + 4, :] = jnp.broadcast_to(row_total, (4, ROWS))
    for d in range(Y_SIZE - 1):
        yt_copy(d, y).start()
        y_copy(d, y).start()
    y_state[y] = row_out[...]
    y_total[y] = rowtot_out[...]
    for d in range(1, Y_SIZE):
        mate = lax.rem(y + d, Y_SIZE)
        y_copy(d - 1, mate).wait_recv()
        yt_copy(d - 1, mate).wait_recv()

    for h in range(2):
        run = jnp.zeros((WIDTH, WIDTH), F32)
        for n in range(Y_SIZE - 1):
            used = (n < y).astype(F32)
            run = jnp.exp(y_total[n, 4 * h : 4 * h + 1, :] * used) * run + (
                y_state[n, h].astype(F32) * used
            )
        for n in range(X_SIZE - 1):
            used = (n < x).astype(F32)
            run = jnp.exp(x_total[n, 4 * h : 4 * h + 1, :] * used) * run + (
                x_state[n, h].astype(F32) * used
            )
        for n in range(CHIPS):
            prefix[n, h] = run.astype(BF16)
            run = chip_share(n, h) * run + state_in[n, h].astype(F32)

    @pl.loop(0, GROUP - 1)
    def _(i):
        p = source(i)
        q_copy(p, p).wait_recv()

    @pl.loop(0, GROUP)
    def _(p):
        chip, core = p // 2, lax.rem(p, 2)
        for h in range(2):
            row = level[pl.ds(2 * p + h, 1), :] + core.astype(F32) * total[pl.ds(4 * chip + h, 1), :]
            _, down = spread(row)
            scaled = (q_in[p, :, h * WIDTH : (h + 1) * WIDTH].astype(F32) * jnp.exp(down)).astype(BF16)
            carried[p, :, h * WIDTH : (h + 1) * WIDTH] = jnp.dot(
                scaled, prefix[chip, h], preferred_element_type=F32
            )

    def out_copy(p):
        return pltpu.make_async_copy(
            result.at[p], out_hbm.at[pl.ds(pl.multiple_of(p * ROWS, ROWS), ROWS), :], out_sem.at[p]
        )

    def finish(p):
        for h in range(2):
            part = slice(h * WIDTH, (h + 1) * WIDTH)
            mixture = carried[p, :, part] + local_in[p, :, part].astype(F32)
            mean_square = jnp.mean(mixture * mixture, axis=1, keepdims=True)
            normed = mixture * lax.rsqrt(mean_square + 1e-06) * gain_ref[:, part]
            result[p, :, part] = normed.astype(BF16)
        out_copy(p).start()

    finish(g)

    @pl.loop(0, GROUP - 1)
    def _(i):
        p = source(i)
        local_copy(p, p).wait_recv()
        finish(p)

    @pl.loop(0, GROUP)
    def _(p):
        out_copy(p).wait()
        sib_copy(p).wait_send()

    @pl.loop(0, GROUP - 1)
    def _(i):
        p = peer(i)
        level_copy(p, g).wait_send()
        q_copy(p, g).wait_send()
        local_copy(p, g).wait_send()

    @pl.loop(1, CHIPS)
    def _(d):
        state_copy(lax.rem(z + d, CHIPS), z).wait_send()

    for d in range(X_SIZE - 1):
        x_copy(d, x).wait_send()
        xt_copy(d, x).wait_send()
    for d in range(Y_SIZE - 1):
        y_copy(d, y).wait_send()
        yt_copy(d, y).wait_send()


def local(queries, keys, values, log_decay, gain):
    chunk_decay = log_decay.reshape(2, GROUP, ROWS).transpose(1, 0, 2).reshape(2 * GROUP, ROWS)
    any_space = pl.BlockSpec(memory_space=pl.ANY)
    vmem = pl.BlockSpec(memory_space=pltpu.VMEM)
    dma = pltpu.SemaphoreType.DMA
    own = pltpu.VMEM((ROWS, GROUP * 2 * WIDTH), BF16)
    tile = pltpu.VMEM((8, ROWS), F32)
    return pl.pallas_call(
        kernel,
        out_shape=jax.ShapeDtypeStruct((GROUP * ROWS, 2 * WIDTH), BF16),
        in_specs=[any_space, any_space, any_space, vmem, vmem],
        out_specs=any_space,
        scratch_shapes=[
            own, own, own,
            pltpu.VMEM((2 * GROUP, ROWS), F32),
            pltpu.VMEM((2 * GROUP, ROWS), F32),
            pltpu.VMEM((CHIPS, 8, ROWS), F32),
            pltpu.VMEM((GROUP, 8, ROWS), F32),
            pltpu.VMEM((GROUP, ROWS, 2 * WIDTH), BF16),
            pltpu.VMEM((GROUP, 2, WIDTH, WIDTH), F32),
            pltpu.VMEM((GROUP, 2, WIDTH, WIDTH), F32),
            pltpu.VMEM((CHIPS, 2, WIDTH, WIDTH), BF16),
            pltpu.VMEM((CHIPS, 2, WIDTH, WIDTH), BF16),
            pltpu.VMEM((GROUP, ROWS, 2 * WIDTH), BF16),
            pltpu.VMEM((GROUP, ROWS, 2 * WIDTH), BF16),
            pltpu.VMEM((2, WIDTH, WIDTH), BF16),
            pltpu.VMEM((X_SIZE, 2, WIDTH, WIDTH), BF16),
            pltpu.VMEM((X_SIZE, 8, ROWS), F32),
            pltpu.VMEM((2, WIDTH, WIDTH), BF16),
            pltpu.VMEM((Y_SIZE, 2, WIDTH, WIDTH), BF16),
            pltpu.VMEM((Y_SIZE, 8, ROWS), F32),
            tile, tile,
            pltpu.VMEM((2, WIDTH, WIDTH), F32),
            pltpu.VMEM((CHIPS, 2, WIDTH, WIDTH), BF16),
            pltpu.VMEM((GROUP, ROWS, 2 * WIDTH), F32),
            pltpu.VMEM((GROUP, ROWS, 2 * WIDTH), BF16),
            dma((4,)),
            dma((GROUP,)), dma((GROUP,)),
            dma((GROUP,)), dma((GROUP,)),
            dma((GROUP,)), dma((GROUP,)),
            dma((CHIPS,)), dma((CHIPS,)),
            dma((GROUP,)), dma((GROUP,)),
            dma((X_SIZE,)), dma((X_SIZE,)), dma((X_SIZE,)), dma((X_SIZE,)),
            dma((Y_SIZE,)), dma((Y_SIZE,)), dma((Y_SIZE,)), dma((Y_SIZE,)),
            dma((GROUP,)),
        ],
        compiler_params=pltpu.CompilerParams(
            collective_id=0, has_side_effects=True, vmem_limit_bytes=60 << 20
        ),
    )(queries, keys, values, chunk_decay, gain.reshape(1, 2 * WIDTH))


def solution(mesh):
    return jax.shard_map(
        local,
        mesh=mesh,
        in_specs=(
            P(("seq", "grp"), None), P(("seq", "grp"), None), P(("seq", "grp"), None),
            P("grp", "seq"), P("grp"),
        ),
        out_specs=P("seq", "grp"),
        check_vma=False,
    )
```

time: 181 us -> 86.5 us (0.48)
  Pallas kernels: 0 us -> 84 us
  local copies, waits for them, and re-layouts: 47.1 us -> 2.26 us
  blocking collectives: 34 us -> 0 us
  starting transfers between devices: 26.5 us -> 0 us
  waiting for transfers between devices: 26.4 us -> 0 us
  matrix products: 22.9 us -> 0 us
  between operations: 14.3 us -> 0.01 us
  other arithmetic: 9.14 us -> 0 us
    pallas_call x0 -> x1, Pallas kernels: none -> 84 us  [local(): pl.pallas_call(kernel, out_shape=jax.ShapeDtypeStruct((GROUP * ROWS, 2 *...]
    all_to_all x3 -> x0, starting transfers between devices: 26.5 us -> none  [the longest x1 11.8 us: local(): lax.all_to_all(keys, 'grp', split_axis=1, concat_axis=0, tiled=True)]
    all_to_all x3 -> x0, waiting for transfers between devices: 26.4 us -> none  [the longest x1 25.7 us: local(): lax.all_to_all(keys, 'grp', split_axis=1, concat_axis=0, tiled=True)]
    slice x32 -> x0, local copies, waits for them, and re-layouts: 25.5 us -> none  [the longest x9 10.6 us: local_mix(): key_heads[:finish]]
    all_gather x2 -> x0, blocking collectives: 25 us -> none  [carried_in(): pieces = jax.tree.map(lambda part: lax.all_gather(part, axis), so_far)]
    dot_general x6 -> x0, matrix products: 22.9 us -> none  [the longest x4 17.7 us: local_mix(): jnp.einsum('hts,shd->thd', weights, value_heads[:finish], preferred_eleme...]
    unnamed x1 -> x0, blocking collectives: 9.03 us -> none
    convert_element_type x4 -> x0, local copies, waits for them, and re-layouts: 6.23 us -> none  [the longest x2 4.39 us: local(): query_heads.astype(jnp.float32) * jnp.exp(levels).T[:, :, None]]
  transfers between devices with their start and end apart: 4 -> 0, of which waited for: 3 -> 0; matrix products, arithmetic and copies ran while one was open for 39% -> 0% of each run, Pallas kernels for 0% -> 0%
where the time goes in v1:
time: 86.5 us; the launch traced here: 86.3 us
  Pallas kernels  84 us (97%)
  local copies, waits for them, and re-layouts  2.26 us (3%)
    pallas_call x1, Pallas kernels, local(): pl.pallas_call(kernel, out_shape=jax.ShapeDtypeStruct((GROUP * ROWS, 2 *...  84 us
    unnamed x1, local copies, waits for them, and re-layouts  2.26 us

profile of v1, /device:TPU:1, one launch (start us, length us, event | category | flops | bytes accessed | tf_op | source)
XLA Modules:
  0.0 86.3 jit_solution(17920405241453229197)
XLA Ops:
  0.0 84.0 %shard_map.55 = bf16[2048,256]{1,0:T(8,128)(2,1)} custom-call(bf16[128,4096]{1,0:T(8,128)(2,1)} %q_hbm.1, bf16[128,4096]{1,0:T(8,128)(2,1)} %k_hbm.1, bf16[128,4096]{1,0:T(8,128)(2,1)} %v_hbm.1, f32[32,128]{1,0:T(8,128)} %bitcast.6, f32[1,256]{1,0:T(1,128)} %bitcast.7), custom_call_target="tpu_custom_call" | custom-call | tf_op jit(solution)/shard_map/pallas_call | solution.py:369
  84.0 2.3 %copy.8 = bf16[2048,256]{1,0:T(8,128)(2,1)} copy(bf16[2048,256]{1,0:T(8,128)(2,1)} %shard_map.55) | data formatting | bytes 2097152

commit v2 on v1

--- a/solution.py
+++ b/solution.py
@@ -25,13 +25,14 @@
 
 
 def kernel(
-    q_hbm, k_hbm, v_hbm, decay_ref, gain_ref, out_hbm,
+    q_hbm, k_hbm, v_hbm, decay_hbm, gain_hbm, out_hbm,
+    decay_ref, gain_ref,
     q_own, k_own, v_own, level, total, level_out, level_in,
     q_in, state_own, state_sib, state_out, state_in, local_out, local_in,
     block_out, x_state, x_total, row_out, y_state, y_total, tot_out, rowtot_out,
-    entering, prefix, carried, result,
+    prefix, carried, result,
     load_sem, level_s, level_r, q_s, q_r, sib_s, sib_r, state_s, state_r, local_s, local_r,
-    x_s, x_r, xt_s, xt_r, y_s, y_r, yt_s, yt_r, out_sem,
+    x_s, x_r, xt_s, xt_r, y_s, y_r, yt_s, yt_r, out_sem, gate,
 ):
     g = lax.axis_index("grp")
     s = lax.axis_index("seq")
@@ -51,27 +52,118 @@
     def cols(p):
         return pl.ds(pl.multiple_of(p * 2 * WIDTH, 2 * WIDTH), 2 * WIDTH)
 
+    barrier = pltpu.get_barrier_semaphore()
+    peers = [peer(i) for i in range(GROUP - 1)]
+    row_mates = [y * X_SIZE + lax.rem(x + d, X_SIZE) for d in range(1, X_SIZE)]
+    column_mates = [lax.rem(y + d, Y_SIZE) * X_SIZE + x for d in range(1, Y_SIZE)]
+    same_core = [lax.rem(z + d, CHIPS) * 2 + c for d in (4, 3, 5, 2, 6, 1, 7)]
+    for p in same_core:
+        pl.semaphore_signal(barrier, inc=1, device_id=(p, s), device_id_type=MESH)
+
+    @pl.when(c == 1)
+    def _():
+        for n in range(CHIPS):
+            pl.semaphore_signal(barrier, inc=1, device_id=(2 * n, s), device_id_type=MESH)
+
+    for m in row_mates + column_mates:
+        pl.semaphore_signal(barrier, inc=1, device_id=(g, m), device_id_type=MESH)
+
+    decay_load = pltpu.make_async_copy(decay_hbm, decay_ref, load_sem.at[4])
+    decay_load.start()
     loads = [
         pltpu.make_async_copy(k_hbm, k_own, load_sem.at[0]),
         pltpu.make_async_copy(v_hbm, v_own, load_sem.at[1]),
         pltpu.make_async_copy(q_hbm, q_own, load_sem.at[2]),
         pltpu.make_async_copy(q_hbm.at[:, cols(g)], q_in.at[g], load_sem.at[3]),
+        pltpu.make_async_copy(gain_hbm, gain_ref, load_sem.at[5]),
     ]
     for copy in loads:
         copy.start()
 
-    barrier = pltpu.get_barrier_semaphore()
-    peers = [peer(i) for i in range(GROUP - 1)]
-    row_mates = [y * X_SIZE + lax.rem(x + d, X_SIZE) for d in range(1, X_SIZE)]
-    column_mates = [lax.rem(y + d, Y_SIZE) * X_SIZE + x for d in range(1, Y_SIZE)]
-    for p in peers:
-        pl.semaphore_signal(barrier, inc=1, device_id=(p, s), device_id_type=MESH)
-    for m in row_mates + column_mates:
-        pl.semaphore_signal(barrier, inc=1, device_id=(g, m), device_id_type=MESH)
+    def level_copy(p, slot):
+        return pltpu.make_async_remote_copy(
+            src_ref=level_out.at[p // 2], dst_ref=level_in.at[slot],
+            send_sem=level_s.at[p], recv_sem=level_r.at[slot],
+            device_id=(p, s), device_id_type=MESH,
+        )
+
+    def q_copy(p, slot):
+        return pltpu.make_async_remote_copy(
+            src_ref=q_hbm.at[:, cols(p)], dst_ref=q_in.at[slot],
+            send_sem=q_s.at[p], recv_sem=q_r.at[slot],
+            device_id=(p, s), device_id_type=MESH,
+        )
+
+    def sib_copy(p):
+        return pltpu.make_async_remote_copy(
+            src_ref=state_own.at[p], dst_ref=state_sib.at[p],
+            send_sem=sib_s.at[p], recv_sem=sib_r.at[p],
+            device_id=(sibling, s), device_id_type=MESH,
+        )
+
+    def state_copy(chip, slot):
+        return pltpu.make_async_remote_copy(
+            src_ref=state_out.at[chip], dst_ref=state_in.at[slot],
+            send_sem=state_s.at[chip], recv_sem=state_r.at[slot],
+            device_id=(chip * 2 + c, s), device_id_type=MESH,
+        )
+
+    def local_copy(p, slot):
+        return pltpu.make_async_remote_copy(
+            src_ref=local_out.at[p], dst_ref=local_in.at[slot],
+            send_sem=local_s.at[p], recv_sem=local_r.at[slot],
+            device_id=(p, s), device_id_type=MESH,
+        )
+
+    def x_copy(d, slot):
+        return pltpu.make_async_remote_copy(
+            src_ref=block_out, dst_ref=x_state.at[slot],
+            send_sem=x_s.at[d], recv_sem=x_r.at[slot],
+            device_id=(g, row_mates[d]), device_id_type=MESH,
+        )
+
+    def xt_copy(d, slot):
+        return pltpu.make_async_remote_copy(
+            src_ref=tot_out, dst_ref=x_total.at[slot],
+            send_sem=xt_s.at[d], recv_sem=xt_r.at[slot],
+            device_id=(g, row_mates[d]), device_id_type=MESH,
+        )
+
+    def y_copy(d, slot):
+        return pltpu.make_async_remote_copy(
+            src_ref=row_out, dst_ref=y_state.at[slot],
+            send_sem=y_s.at[d], recv_sem=y_r.at[slot],
+            device_id=(g, column_mates[d]), device_id_type=MESH,
+        )
+
+    def yt_copy(d, slot):
+        return pltpu.make_async_remote_copy(
+            src_ref=rowtot_out, dst_ref=y_total.at[slot],
+            send_sem=yt_s.at[d], recv_sem=yt_r.at[slot],
+            device_id=(g, column_mates[d]), device_id_type=MESH,
+        )
+
+    greeters = len(same_core) + len(row_mates) + len(column_mates)
+    far = [lax.rem(z + d, CHIPS) * 2 for d in (4, 3, 5)]
+    near = [lax.rem(z + d, CHIPS) * 2 for d in (2, 6, 1, 7)]
+
+    @pl.when(c == 0)
+    def _():
+        pl.semaphore_wait(barrier, greeters + CHIPS)
+        for n in range(CHIPS):
+            pl.semaphore_signal(gate, inc=1, device_id=(2 * n + 1, s), device_id_type=MESH)
+        q_copy(far[0], g).start()
+        q_copy(far[0] + 1, g).start()
+
+    @pl.when(c == 1)
+    def _():
+        pl.semaphore_wait(barrier, greeters)
+        q_copy(same_core[0], g).start()
 
     here = lax.broadcasted_iota(jnp.int32, (ROWS, ROWS), 0)
     there = lax.broadcasted_iota(jnp.int32, (ROWS, ROWS), 1)
     upto = (here <= there).astype(F32)
+    decay_load.wait()
     chunk_levels = jnp.dot(
         decay_ref[...], upto, preferred_element_type=F32, precision=lax.Precision.HIGHEST
     )
@@ -89,85 +181,38 @@
     level_in[g] = level_out[z]
     x_total[x] = tot_out[...]
 
-    pl.semaphore_wait(barrier, len(peers) + len(row_mates) + len(column_mates))
-
-    def level_copy(p, slot):
-        return pltpu.make_async_remote_copy(
-            src_ref=level_out.at[p // 2], dst_ref=level_in.at[slot],
-            send_sem=level_s.at[p], recv_sem=level_r.at[slot],
-            device_id=(p, s), device_id_type=MESH,
-        )
-
-    def q_copy(p, slot):
-        return pltpu.make_async_remote_copy(
-            src_ref=q_hbm.at[:, cols(p)], dst_ref=q_in.at[slot],
-            send_sem=q_s.at[p], recv_sem=q_r.at[slot],
-            device_id=(p, s), device_id_type=MESH,
-        )
-
-    def sib_copy(p):
-        return pltpu.make_async_remote_copy(
-            src_ref=state_own.at[p], dst_ref=state_sib.at[p],
-            send_sem=sib_s.at[p], recv_sem=sib_r.at[p],
-            device_id=(sibling, s), device_id_type=MESH,
-        )
-
-    def state_copy(chip, slot):
-        return pltpu.make_async_remote_copy(
-            src_ref=state_out.at[chip], dst_ref=state_in.at[slot],
-            send_sem=state_s.at[chip], recv_sem=state_r.at[slot],
-            device_id=(chip * 2 + c, s), device_id_type=MESH,
-        )
-
-    def local_copy(p, slot):
-        return pltpu.make_async_remote_copy(
-            src_ref=local_out.at[p], dst_ref=local_in.at[slot],
-            send_sem=local_s.at[p], recv_sem=local_r.at[slot],
-            device_id=(p, s), device_id_type=MESH,
-        )
-
-    def x_copy(d, slot):
-        return pltpu.make_async_remote_copy(
-            src_ref=block_out, dst_ref=x_state.at[slot],
-            send_sem=x_s.at[d], recv_sem=x_r.at[slot],
-            device_id=(g, row_mates[d]), device_id_type=MESH,
-        )
-
-    def xt_copy(d, slot):
-        return pltpu.make_async_remote_copy(
-            src_ref=tot_out, dst_ref=x_total.at[slot],
-            send_sem=xt_s.at[d], recv_sem=xt_r.at[slot],
-            device_id=(g, row_mates[d]), device_id_type=MESH,
-        )
-
-    def y_copy(d, slot):
-        return pltpu.make_async_remote_copy(
-            src_ref=row_out, dst_ref=y_state.at[slot],
-            send_sem=y_s.at[d], recv_sem=y_r.at[slot],
-            device_id=(g, column_mates[d]), device_id_type=MESH,
-        )
-
-    def yt_copy(d, slot):
-        return pltpu.make_async_remote_copy(
-            src_ref=rowtot_out, dst_ref=y_total.at[slot],
-            send_sem=yt_s.at[d], recv_sem=yt_r.at[slot],
-            device_id=(g, column_mates[d]), device_id_type=MESH,
-        )
-
-    for p in peers:
-        level_copy(p, g).start()
-    for d in range(X_SIZE - 1):
-        xt_copy(d, x).start()
-    for p in peers:
-        q_copy(p, g).start()
+
+    @pl.when(c == 0)
+    def _():
+        for p in same_core:
+            level_copy(p, g).start()
+        for n in range(CHIPS):
+            level_copy(2 * n + 1, g).start()
+        for d in range(X_SIZE - 1):
+            xt_copy(d, x).start()
+        for p in far[1:]:
+            q_copy(p, g).start()
+            q_copy(p + 1, g).start()
+
+    @pl.when(c == 1)
+    def _():
+        for p in same_core:
+            level_copy(p, g).start()
+        for d in range(X_SIZE - 1):
+            xt_copy(d, x).start()
+        for p in same_core[1:]:
+            q_copy(p, g).start()
+        pl.semaphore_wait(gate, CHIPS)
+        for n in range(CHIPS):
+            level_copy(2 * n, g).start()
+        for p in far:
+            q_copy(p, g).start()
 
     for copy in loads:
         copy.wait()
 
-    @pl.loop(0, GROUP - 1)
-    def _(i):
-        p = source(i)
-        level_copy(p, p).wait_recv()
+    def owner(i):
+        return lax.rem(z + order(2 * lax.rem(i, CHIPS))[0], CHIPS) * 2 + i // CHIPS
 
     def spread(row):
         wide = jnp.broadcast_to(row, (ROWS, ROWS))
@@ -178,7 +223,12 @@
 
     @pl.loop(0, GROUP)
     def _(i):
-        p = peer(i)
+        p = owner(i)
+
+        @pl.when(p != g)
+        def _():
+            level_copy(p, p).wait_recv()
+
         for h in range(2):
             _, down = spread(level_in[p, pl.ds(2 * c + h, 1), :])
             tail = jnp.exp(down[ROWS - 1 : ROWS, :] - down)
@@ -191,7 +241,7 @@
 
     @pl.loop(0, GROUP)
     def _(i):
-        p = peer(i)
+        p = owner(i)
         sib_copy(p).wait_recv()
 
         @pl.when(lax.rem(p, 2) == c)
@@ -204,13 +254,26 @@
                 )
                 state_out[p // 2, h] = merged.astype(BF16)
 
-            @pl.when(i < GROUP - 1)
+            @pl.when(p != g)
             def _():
                 state_copy(p // 2, z).start()
 
-            @pl.when(i == GROUP - 1)
+            @pl.when(p == g)
             def _():
                 state_in[z] = state_out[z]
+
+    @pl.when(c == 0)
+    def _():
+        for p in near:
+            q_copy(p, g).start()
+            q_copy(p + 1, g).start()
+        q_copy(sibling, g).start()
+
+    @pl.when(c == 1)
+    def _():
+        for p in near:
+            q_copy(p, g).start()
+        q_copy(sibling, g).start()
 
     causal = here >= there
 
@@ -329,15 +392,8 @@
 
     finish(g)
 
-    @pl.loop(0, GROUP - 1)
-    def _(i):
-        p = source(i)
-        local_copy(p, p).wait_recv()
-        finish(p)
-
     @pl.loop(0, GROUP)
     def _(p):
-        out_copy(p).wait()
         sib_copy(p).wait_send()
 
     @pl.loop(0, GROUP - 1)
@@ -345,7 +401,6 @@
         p = peer(i)
         level_copy(p, g).wait_send()
         q_copy(p, g).wait_send()
-        local_copy(p, g).wait_send()
 
     @pl.loop(1, CHIPS)
     def _(d):
@@ -358,20 +413,32 @@
         y_copy(d, y).wait_send()
         yt_copy(d, y).wait_send()
 
+    @pl.loop(0, GROUP - 1)
+    def _(i):
+        p = source(i)
+        local_copy(peer(i), g).wait_send()
+        local_copy(p, p).wait_recv()
+        finish(p)
+
+    @pl.loop(0, GROUP)
+    def _(p):
+        out_copy(p).wait()
+
 
 def local(queries, keys, values, log_decay, gain):
     chunk_decay = log_decay.reshape(2, GROUP, ROWS).transpose(1, 0, 2).reshape(2 * GROUP, ROWS)
     any_space = pl.BlockSpec(memory_space=pl.ANY)
-    vmem = pl.BlockSpec(memory_space=pltpu.VMEM)
     dma = pltpu.SemaphoreType.DMA
     own = pltpu.VMEM((ROWS, GROUP * 2 * WIDTH), BF16)
     tile = pltpu.VMEM((8, ROWS), F32)
     return pl.pallas_call(
         kernel,
         out_shape=jax.ShapeDtypeStruct((GROUP * ROWS, 2 * WIDTH), BF16),
-        in_specs=[any_space, any_space, any_space, vmem, vmem],
+        in_specs=[any_space] * 5,
         out_specs=any_space,
         scratch_shapes=[
+            pltpu.VMEM((2 * GROUP, ROWS), F32),
+            pltpu.VMEM((1, 2 * WIDTH), F32),
             own, own, own,
             pltpu.VMEM((2 * GROUP, ROWS), F32),
             pltpu.VMEM((2 * GROUP, ROWS), F32),
@@ -391,11 +458,10 @@
             pltpu.VMEM((Y_SIZE, 2, WIDTH, WIDTH), BF16),
             pltpu.VMEM((Y_SIZE, 8, ROWS), F32),
             tile, tile,
-            pltpu.VMEM((2, WIDTH, WIDTH), F32),
             pltpu.VMEM((CHIPS, 2, WIDTH, WIDTH), BF16),
             pltpu.VMEM((GROUP, ROWS, 2 * WIDTH), F32),
             pltpu.VMEM((GROUP, ROWS, 2 * WIDTH), BF16),
-            dma((4,)),
+            dma((6,)),
             dma((GROUP,)), dma((GROUP,)),
             dma((GROUP,)), dma((GROUP,)),
             dma((GROUP,)), dma((GROUP,)),
@@ -404,6 +470,7 @@
             dma((X_SIZE,)), dma((X_SIZE,)), dma((X_SIZE,)), dma((X_SIZE,)),
             dma((Y_SIZE,)), dma((Y_SIZE,)), dma((Y_SIZE,)), dma((Y_SIZE,)),
             dma((GROUP,)),
+            pltpu.SemaphoreType.REGULAR,
         ],
         compiler_params=pltpu.CompilerParams(
             collective_id=0, has_side_effects=True, vmem_limit_bytes=60 << 20

time: 86.5 us -> 79.8 us (0.923)
  Pallas kernels: 84 us -> 77.3 us
    pallas_call x1, Pallas kernels: 84 us -> 77.3 us  [local(): pl.pallas_call(kernel, out_shape=jax.ShapeDtypeStruct((GROUP * ROWS, 2 *...]
where the time goes in v2:
time: 79.8 us; the launch traced here: 79.6 us
  Pallas kernels  77.3 us (97%)
  local copies, waits for them, and re-layouts  2.26 us (3%)
    pallas_call x1, Pallas kernels, local(): pl.pallas_call(kernel, out_shape=jax.ShapeDtypeStruct((GROUP * ROWS, 2 *...  77.3 us
    unnamed x1, local copies, waits for them, and re-layouts  2.26 us

profile of v2, /device:TPU:1, one launch (start us, length us, event | category | flops | bytes accessed | tf_op | source)
XLA Modules:
  0.0 79.6 jit_solution(1248020261239997635)
XLA Ops:
  0.0 77.3 %shard_map.55 = bf16[2048,256]{1,0:T(8,128)(2,1)} custom-call(bf16[128,4096]{1,0:T(8,128)(2,1)} %q_hbm.1, bf16[128,4096]{1,0:T(8,128)(2,1)} %k_hbm.1, bf16[128,4096]{1,0:T(8,128)(2,1)} %v_hbm.1, f32[32,128]{1,0:T(8,128)} %bitcast.6, f32[1,256]{1,0:T(1,128)} %bitcast.7), custom_call_target="tpu_custom_call" | custom-call | tf_op jit(solution)/shard_map/pallas_call | solution.py:434
  77.4 2.3 %copy.8 = bf16[2048,256]{1,0:T(8,128)(2,1)} copy(bf16[2048,256]{1,0:T(8,128)(2,1)} %shard_map.55) | data formatting | bytes 2097152

commit v3 on v2

v3 whole, which is shorter than its diff:
```python
import jax
import jax.numpy as jnp
from jax import lax
from jax.experimental import pallas as pl
from jax.experimental.pallas import tpu as pltpu
from jax.sharding import PartitionSpec as P

MESH = pl.DeviceIdType.MESH
F32 = jnp.float32
BF16 = jnp.bfloat16
CHIPS = 8
GROUP = 16
ROWS = 128
WIDTH = 128
X_SIZE = 4
Y_SIZE = 8
KEPT, SENT = 1, 0


def order(i):
    m = i // 2
    odd = m % 2
    return 4 + (1 - 2 * odd) * ((m + 1) // 2), 1 - i % 2


def kernel(
    q_hbm, k_hbm, v_hbm, decay_hbm, gain_hbm, out_hbm,
    decay_ref, gain_ref,
    q_own, k_own, v_own, level, total, level_out, level_in,
    q_in, state_own, state_sib, state_out, state_in, local_out, local_in, local_kept,
    block_out, x_state, x_total, row_out, y_state, y_total, tot_out, rowtot_out,
    prefix, entering, carried, result, result_kept,
    load_sem, level_s, level_r, q_s, q_r, sib_s, sib_r, state_s, state_r, local_s, local_r,
    x_s, x_r, xt_s, xt_r, y_s, y_r, yt_s, yt_r, enter_s, enter_r, pass_s, done_s, done_r,
    out_sem, hand_s, gate, sib_gate,
):
    g = lax.axis_index("grp")
    s = lax.axis_index("seq")
    z, c = g // 2, lax.rem(g, 2)
    y, x = s // X_SIZE, lax.rem(s, X_SIZE)
    cf = c.astype(F32)
    sibling = g + 1 - 2 * c

    def peer(i):
        dz, dc = order(i)
        return lax.rem(z + dz, CHIPS) * 2 + lax.rem(c + dc, 2)

    def source(i):
        dz, dc = order(i)
        return lax.rem(z + 2 * CHIPS - dz, CHIPS) * 2 + lax.rem(c + dc, 2)

    def cols(p, h):
        return pl.ds(pl.multiple_of(p * 2 * WIDTH + h * WIDTH, WIDTH), WIDTH)

    def rows(p):
        return pl.ds(pl.multiple_of(p * ROWS, ROWS), ROWS)

    def side(h):
        return pl.ds(h * WIDTH, WIDTH)

    barrier = pltpu.get_barrier_semaphore()
    row_mates = [y * X_SIZE + lax.rem(x + d, X_SIZE) for d in range(1, X_SIZE)]
    column_mates = [lax.rem(y + d, Y_SIZE) * X_SIZE + x for d in range(1, Y_SIZE)]
    same_core = [lax.rem(z + d, CHIPS) * 2 + c for d in (4, 3, 5, 2, 6, 1, 7)]
    zeros = [lax.rem(z + d, CHIPS) * 2 for d in (4, 3, 5, 2, 6, 1, 7)]
    for p in same_core:
        pl.semaphore_signal(barrier, inc=1, device_id=(p, s), device_id_type=MESH)

    @pl.when(c == 1)
    def _():
        for n in range(CHIPS):
            pl.semaphore_signal(barrier, inc=1, device_id=(2 * n, s), device_id_type=MESH)

    for m in row_mates + column_mates:
        pl.semaphore_signal(barrier, inc=1, device_id=(g, m), device_id_type=MESH)
    greeters = len(same_core) + len(row_mates) + len(column_mates)

    decay_load = pltpu.make_async_copy(decay_hbm, decay_ref, load_sem.at[0])
    gain_load = pltpu.make_async_copy(gain_hbm, gain_ref, load_sem.at[1])
    loads = [
        pltpu.make_async_copy(k_hbm, k_own, load_sem.at[2]),
        pltpu.make_async_copy(v_hbm, v_own, load_sem.at[3]),
        pltpu.make_async_copy(q_hbm, q_own, load_sem.at[4]),
        pltpu.make_async_copy(q_hbm.at[:, cols(g, SENT)], q_in.at[g], load_sem.at[5]),
    ]
    for copy in [decay_load, gain_load] + loads:
        copy.start()

    def level_copy(p, slot):
        return pltpu.make_async_remote_copy(
            src_ref=level_out.at[p // 2], dst_ref=level_in.at[slot],
            send_sem=level_s.at[p], recv_sem=level_r.at[slot],
            device_id=(p, s), device_id_type=MESH,
        )

    def hand_copy(p):
        return pltpu.make_async_remote_copy(
            src_ref=level_in.at[p], dst_ref=level_in.at[p],
            send_sem=hand_s.at[p], recv_sem=level_r.at[p],
            device_id=(sibling, s), device_id_type=MESH,
        )

    def q_copy(p, slot):
        return pltpu.make_async_remote_copy(
            src_ref=q_hbm.at[:, cols(p, SENT)], dst_ref=q_in.at[slot],
            send_sem=q_s.at[p], recv_sem=q_r.at[slot],
            device_id=(p, s), device_id_type=MESH,
        )

    def sib_copy(p):
        return pltpu.make_async_remote_copy(
            src_ref=state_own.at[p], dst_ref=state_sib.at[p],
            send_sem=sib_s.at[p], recv_sem=sib_r.at[p],
            device_id=(sibling, s), device_id_type=MESH,
        )

    def state_copy(h, chip, slot):
        return pltpu.make_async_remote_copy(
            src_ref=state_out.at[h, chip], dst_ref=state_in.at[h, slot],
            send_sem=state_s.at[h, chip], recv_sem=state_r.at[h, slot],
            device_id=(chip * 2 + c, s), device_id_type=MESH,
        )

    def local_copy(p, slot):
        return pltpu.make_async_remote_copy(
            src_ref=local_out.at[p], dst_ref=local_in.at[slot],
            send_sem=local_s.at[p], recv_sem=local_r.at[slot],
            device_id=(p, s), device_id_type=MESH,
        )

    def x_copy(h, d, slot):
        return pltpu.make_async_remote_copy(
            src_ref=block_out.at[h], dst_ref=x_state.at[h, slot],
            send_sem=x_s.at[h, d], recv_sem=x_r.at[h, slot],
            device_id=(g, row_mates[d]), device_id_type=MESH,
        )

    def xt_copy(d, slot):
        return pltpu.make_async_remote_copy(
            src_ref=tot_out, dst_ref=x_total.at[slot],
            send_sem=xt_s.at[d], recv_sem=xt_r.at[slot],
            device_id=(g, row_mates[d]), device_id_type=MESH,
        )

    def y_copy(h, d, slot):
        return pltpu.make_async_remote_copy(
            src_ref=row_out.at[h], dst_ref=y_state.at[h, slot],
            send_sem=y_s.at[h, d], recv_sem=y_r.at[h, slot],
            device_id=(g, column_mates[d]), device_id_type=MESH,
        )

    def yt_copy(d, slot):
        return pltpu.make_async_remote_copy(
            src_ref=rowtot_out, dst_ref=y_total.at[slot],
            send_sem=yt_s.at[d], recv_sem=yt_r.at[slot],
            device_id=(g, column_mates[d]), device_id_type=MESH,
        )

    def enter_copy(chip, slot):
        return pltpu.make_async_remote_copy(
            src_ref=prefix.at[KEPT, chip], dst_ref=entering.at[slot],
            send_sem=enter_s.at[chip], recv_sem=enter_r.at[slot],
            device_id=(chip * 2 + c, s), device_id_type=MESH,
        )

    def pass_copy(p):
        return pltpu.make_async_remote_copy(
            src_ref=entering.at[p], dst_ref=entering.at[p],
            send_sem=pass_s.at[p], recv_sem=enter_r.at[p],
            device_id=(sibling, s), device_id_type=MESH,
        )

    def done_copy(p, slot):
        return pltpu.make_async_remote_copy(
            src_ref=result_kept.at[p], dst_ref=out_hbm.at[rows(slot), side(KEPT)],
            send_sem=done_s.at[p], recv_sem=done_r.at[slot],
            device_id=(p, s), device_id_type=MESH,
        )

    @pl.when(c == 0)
    def _():
        pl.semaphore_wait(barrier, greeters + CHIPS)
        pl.semaphore_signal(sib_gate, inc=1, device_id=(sibling, s), device_id_type=MESH)
        for n in range(CHIPS):
            pl.semaphore_signal(gate, inc=1, device_id=(2 * n + 1, s), device_id_type=MESH)
        q_copy(zeros[0], g).start()
        q_copy(zeros[0] + 1, g).start()

    @pl.when(c == 1)
    def _():
        pl.semaphore_wait(barrier, greeters)
        q_copy(same_core[0], g).start()

    here = lax.broadcasted_iota(jnp.int32, (ROWS, ROWS), 0)
    there = lax.broadcasted_iota(jnp.int32, (ROWS, ROWS), 1)
    upto = (here <= there).astype(F32)
    decay_load.wait()
    gain_load.wait()
    chunk_levels = jnp.dot(
        decay_ref[...], upto, preferred_element_type=F32, precision=lax.Precision.HIGHEST
    )
    chunk_totals = jnp.broadcast_to(chunk_levels[:, ROWS - 1 : ROWS], (2 * GROUP, ROWS))
    level[...] = chunk_levels
    total[...] = chunk_totals
    gain_kept = jnp.broadcast_to(gain_ref[:, KEPT * WIDTH : (KEPT + 1) * WIDTH], (4, WIDTH))
    for n in range(CHIPS):
        level_out[n, 0:4, :] = chunk_levels[4 * n : 4 * n + 4]
        level_out[n, 4:8, :] = gain_kept
    for h in range(2):
        block_total = chunk_totals[h : h + 1]
        for n in range(1, GROUP):
            block_total = block_total + chunk_totals[2 * n + h : 2 * n + h + 1]
        tot_out[4 * h : 4 * h + 4, :] = jnp.broadcast_to(block_total, (4, ROWS))
    level_in[g] = level_out[z]
    x_total[x] = tot_out[...]

    @pl.when(c == 0)
    def _():
        for p in same_core:
            level_copy(p, g).start()
        for n in range(CHIPS):
            level_copy(2 * n + 1, g).start()
        for d in range(X_SIZE - 1):
            xt_copy(d, x).start()
        for p in zeros[1:]:
            q_copy(p, g).start()
            q_copy(p + 1, g).start()
        q_copy(sibling, g).start()

    @pl.when(c == 1)
    def _():
        for p in same_core:
            level_copy(p, g).start()
        for d in range(X_SIZE - 1):
            xt_copy(d, x).start()
        for p in same_core[1:3]:
            q_copy(p, g).start()
        for p in same_core:
            level_copy(p, p).wait_recv()
        pl.semaphore_wait(sib_gate, 1)
        for n in range(CHIPS):
            hand_copy(2 * n + 1).start()
        for p in same_core[3:]:
            q_copy(p, g).start()
        pl.semaphore_wait(gate, CHIPS)
        for p in zeros:
            q_copy(p, g).start()
        q_copy(sibling, g).start()

    for copy in loads:
        copy.wait()

    def owner(i):
        return lax.rem(z + order(2 * lax.rem(i, CHIPS))[0], CHIPS) * 2 + 1 - i // CHIPS

    def chip_at(i):
        return lax.rem(z + order(2 * i)[0], CHIPS)

    def spread(row):
        wide = jnp.broadcast_to(row, (ROWS, ROWS))
        return wide, wide.T

    @pl.loop(0, GROUP)
    def _(i):
        p = owner(i)

        @pl.when(jnp.logical_or(
            jnp.logical_and(c == 0, p != g), jnp.logical_and(c == 1, lax.rem(p, 2) == 0)
        ))
        def _():
            level_copy(p, p).wait_recv()

        for h in range(2):
            _, down = spread(level_in[p, pl.ds(2 * c + h, 1), :])
            tail = jnp.exp(down[ROWS - 1 : ROWS, :] - down)
            scaled = (k_own[:, cols(p, h)].astype(F32) * tail).astype(BF16)
            state_own[p, h] = lax.dot_general(
                scaled, v_own[:, cols(p, h)], (((0,), (0,)), ((), ())),
                preferred_element_type=F32,
            )
        sib_copy(p).start()

    @pl.loop(0, GROUP)
    def _(i):
        sib_copy(owner(i)).wait_recv()

    for h in (KEPT, SENT):
        @pl.loop(0, CHIPS)
        def _(i):
            chip = chip_at(i)
            p = chip * 2 + c
            late = jnp.broadcast_to(level_in[p, 2 + h : 3 + h, ROWS - 1 : ROWS], (1, WIDTH))
            merged = (
                jnp.exp(late * (1.0 - cf)) * state_own[p, h]
                + jnp.exp(late * cf) * state_sib[p, h]
            )
            state_out[h, chip] = merged.astype(BF16)

            @pl.when(i < CHIPS - 1)
            def _():
                state_copy(h, chip, z).start()

            @pl.when(i == CHIPS - 1)
            def _():
                state_in[h, z] = state_out[h, z]

    causal = here >= there

    def inside(p, h):
        wide, down = spread(level_in[p, pl.ds(2 * c + h, 1), :])
        q_head = q_own[:, cols(p, h)]
        scores = lax.dot_general(
            q_head, k_own[:, cols(p, h)], (((1,), (1,)), ((), ())),
            preferred_element_type=F32,
        )
        gap = jnp.where(causal, down - wide, 0.0)
        weights = jnp.where(causal, scores * jnp.exp(gap), 0.0).astype(BF16)
        part = jnp.dot(weights, v_own[:, cols(p, h)], preferred_element_type=F32)
        scaled = (q_head.astype(F32) * (jnp.exp(down) * cf)).astype(BF16)
        return part + jnp.dot(
            scaled, state_sib[p, h].astype(BF16), preferred_element_type=F32
        )

    @pl.loop(0, GROUP)
    def _(i):
        p = peer(i)
        local_out[p] = inside(p, SENT).astype(BF16)

        @pl.when(i < GROUP - 1)
        def _():
            local_copy(p, g).start()

        @pl.when(i == GROUP - 1)
        def _():
            local_in[g] = local_out[g]

    @pl.loop(0, GROUP)
    def _(p):
        local_kept[p] = inside(p, KEPT)

    def chip_share(n, h):
        return jnp.exp(total[4 * n + h : 4 * n + h + 1, :] + total[4 * n + 2 + h : 4 * n + 3 + h, :])

    def send_block(h):
        @pl.loop(1, CHIPS)
        def _(d):
            chip = lax.rem(z + d, CHIPS)
            state_copy(h, chip, chip).wait_recv()

        run = state_in[h, 0].astype(F32)
        for n in range(1, CHIPS):
            run = chip_share(n, h) * run + state_in[h, n].astype(F32)
        block_out[h] = run.astype(BF16)
        for d in range(X_SIZE - 1):
            x_copy(h, d, x).start()
        x_state[h, x] = block_out[h]

    def send_row(h):
        for d in range(1, X_SIZE):
            x_copy(h, d - 1, lax.rem(x + d, X_SIZE)).wait_recv()
        run = x_state[h, 0].astype(F32)
        for n in range(1, X_SIZE):
            run = jnp.exp(x_total[n, 4 * h : 4 * h + 1, :]) * run + x_state[h, n].astype(F32)
        row_out[h] = run.astype(BF16)
        for d in range(Y_SIZE - 1):
            y_copy(h, d, y).start()
        y_state[h, y] = row_out[h]

    def enter(h):
        for d in range(Y_SIZE - 1):
            y_copy(h, d, lax.rem(y + d + 1, Y_SIZE)).wait_recv()
        run = jnp.zeros((WIDTH, WIDTH), F32)
        for n in range(Y_SIZE - 1):
            used = (n < y).astype(F32)
            run = jnp.exp(y_total[n, 4 * h : 4 * h + 1, :] * used) * run + (
                y_state[h, n].astype(F32) * used
            )
        for n in range(X_SIZE - 1):
            used = (n < x).astype(F32)
            run = jnp.exp(x_total[n, 4 * h : 4 * h + 1, :] * used) * run + (
                x_state[h, n].astype(F32) * used
            )
        for n in range(CHIPS):
            prefix[h, n] = run.astype(BF16)
            run = chip_share(n, h) * run + state_in[h, n].astype(F32)

    for d in range(1, X_SIZE):
        xt_copy(d - 1, lax.rem(x + d, X_SIZE)).wait_recv()
    for h in range(2):
        row_total = x_total[0, 4 * h : 4 * h + 1, :]
        for n in range(1, X_SIZE):
            row_total = row_total + x_total[n, 4 * h : 4 * h + 1, :]
        rowtot_out[4 * h : 4 * h + 4, :] = jnp.broadcast_to(row_total, (4, ROWS))
    for d in range(Y_SIZE - 1):
        yt_copy(d, y).start()
    y_total[y] = rowtot_out[...]

    send_block(KEPT)
    for d in range(Y_SIZE - 1):
        yt_copy(d, lax.rem(y + d + 1, Y_SIZE)).wait_recv()
    send_row(KEPT)
    send_block(SENT)
    enter(KEPT)

    @pl.loop(0, CHIPS - 1)
    def _(i):
        enter_copy(chip_at(i), g).start()

    entering[g] = prefix[KEPT, z]
    send_row(SENT)

    def finish_kept(p):
        row = level_in[p, pl.ds(2 * c + KEPT, 1), :] + cf * jnp.broadcast_to(
            level_in[p, KEPT : KEPT + 1, ROWS - 1 : ROWS], (1, ROWS)
        )
        _, down = spread(row)
        scaled = (q_own[:, cols(p, KEPT)].astype(F32) * jnp.exp(down)).astype(BF16)
        mixture = local_kept[p] + jnp.dot(scaled, entering[p], preferred_element_type=F32)
        mean_square = jnp.mean(mixture * mixture, axis=1, keepdims=True)
        normed = mixture * lax.rsqrt(mean_square + 1e-06) * level_in[p, 4:5, :]
        result_kept[p] = normed.astype(BF16)

    def own_done():
        return pltpu.make_async_copy(
            result_kept.at[g], out_hbm.at[rows(g), side(KEPT)], done_s.at[g]
        )

    pass_copy(g).start()

    @pl.loop(0, CHIPS - 1)
    def _(i):
        p = lax.rem(z + 2 * CHIPS - order(2 * i)[0], CHIPS) * 2 + c
        enter_copy(0, p).wait_recv()
        pass_copy(p).start()
        finish_kept(p)
        done_copy(p, g).start()

    @pl.loop(0, CHIPS)
    def _(i):
        p = lax.rem(z + 2 * CHIPS - order(2 * i)[0], CHIPS) * 2 + 1 - c
        pass_copy(p).wait_recv()
        finish_kept(p)
        done_copy(p, g).start()

    finish_kept(g)
    own_done().start()

    enter(SENT)

    @pl.loop(0, GROUP - 1)
    def _(i):
        p = source(i)
        q_copy(p, p).wait_recv()

    @pl.loop(0, GROUP)
    def _(p):
        chip, core = p // 2, lax.rem(p, 2)
        row = level[pl.ds(2 * p + SENT, 1), :] + (
            core.astype(F32) * total[pl.ds(4 * chip + SENT, 1), :]
        )
        _, down = spread(row)
        scaled = (q_in[p].astype(F32) * jnp.exp(down)).astype(BF16)
        carried[p] = jnp.dot(scaled, prefix[SENT, chip], preferred_element_type=F32)

    def out_copy(p):
        return pltpu.make_async_copy(
            result.at[p], out_hbm.at[rows(p), side(SENT)], out_sem.at[p]
        )

    def finish_sent(p):
        mixture = carried[p] + local_in[p].astype(F32)
        mean_square = jnp.mean(mixture * mixture, axis=1, keepdims=True)
        normed = mixture * lax.rsqrt(mean_square + 1e-06) * gain_ref[:, 0:WIDTH]
        result[p] = normed.astype(BF16)
        out_copy(p).start()

    finish_sent(g)

    @pl.loop(0, GROUP - 1)
    def _(i):
        p = source(i)
        local_copy(p, p).wait_recv()
        finish_sent(p)

    @pl.loop(0, GROUP)
    def _(p):
        sib_copy(p).wait_send()

    @pl.loop(0, GROUP - 1)
    def _(i):
        p = peer(i)

        @pl.when(jnp.logical_or(c == 0, lax.rem(p, 2) == 1))
        def _():
            level_copy(p, g).wait_send()

        q_copy(p, g).wait_send()
        local_copy(p, g).wait_send()

    @pl.when(c == 1)
    def _():
        for n in range(CHIPS):
            hand_copy(2 * n + 1).wait_send()

    for h in range(2):
        @pl.loop(0, CHIPS - 1)
        def _(i):
            state_copy(h, chip_at(i), z).wait_send()

        for d in range(X_SIZE - 1):
            x_copy(h, d, x).wait_send()
        for d in range(Y_SIZE - 1):
            y_copy(h, d, y).wait_send()

    @pl.loop(0, CHIPS - 1)
    def _(i):
        enter_copy(chip_at(i), g).wait_send()

    @pl.loop(0, CHIPS)
    def _(n):
        pass_copy(2 * n + c).wait_send()

    for d in range(X_SIZE - 1):
        xt_copy(d, x).wait_send()
    for d in range(Y_SIZE - 1):
        yt_copy(d, y).wait_send()
    own_done().wait()

    @pl.loop(0, GROUP)
    def _(p):
        out_copy(p).wait()

    @pl.loop(0, GROUP - 1)
    def _(i):
        p = source(i)
        done_copy(peer(i), g).wait_send()
        done_copy(p, p).wait_recv()


def local(queries, keys, values, log_decay, gain):
    chunk_decay = log_decay.reshape(2, GROUP, ROWS).transpose(1, 0, 2).reshape(2 * GROUP, ROWS)
    any_space = pl.BlockSpec(memory_space=pl.ANY)
    dma = pltpu.SemaphoreType.DMA
    own = pltpu.VMEM((ROWS, GROUP * 2 * WIDTH), BF16)
    tile = pltpu.VMEM((8, ROWS), F32)

    def parts(*lead):
        return pltpu.VMEM((*lead, ROWS, WIDTH), BF16)

    def wide_parts(*lead):
        return pltpu.VMEM((*lead, ROWS, WIDTH), F32)

    return pl.pallas_call(
        kernel,
        out_shape=jax.ShapeDtypeStruct((GROUP * ROWS, 2 * WIDTH), BF16),
        in_specs=[any_space] * 5,
        out_specs=any_space,
        scratch_shapes=[
            pltpu.VMEM((2 * GROUP, ROWS), F32),
            pltpu.VMEM((1, 2 * WIDTH), F32),
            own, own, own,
            pltpu.VMEM((2 * GROUP, ROWS), F32),
            pltpu.VMEM((2 * GROUP, ROWS), F32),
            pltpu.VMEM((CHIPS, 8, ROWS), F32),
            pltpu.VMEM((GROUP, 8, ROWS), F32),
            parts(GROUP),
            wide_parts(GROUP, 2), wide_parts(GROUP, 2),
            parts(2, CHIPS), parts(2, CHIPS),
            parts(GROUP), parts(GROUP), wide_parts(GROUP),
            parts(2), parts(2, X_SIZE),
            pltpu.VMEM((X_SIZE, 8, ROWS), F32),
            parts(2), parts(2, Y_SIZE),
            pltpu.VMEM((Y_SIZE, 8, ROWS), F32),
            tile, tile,
            parts(2, CHIPS), parts(GROUP), wide_parts(GROUP), parts(GROUP), parts(GROUP),
            dma((6,)),
            dma((GROUP,)), dma((GROUP,)),
            dma((GROUP,)), dma((GROUP,)),
            dma((GROUP,)), dma((GROUP,)),
            dma((2, CHIPS)), dma((2, CHIPS)),
            dma((GROUP,)), dma((GROUP,)),
            dma((2, X_SIZE)), dma((2, X_SIZE)), dma((X_SIZE,)), dma((X_SIZE,)),
            dma((2, Y_SIZE)), dma((2, Y_SIZE)), dma((Y_SIZE,)), dma((Y_SIZE,)),
            dma((CHIPS,)), dma((GROUP,)), dma((GROUP,)), dma((GROUP,)), dma((GROUP,)),
            dma((GROUP,)), dma((GROUP,)),
            pltpu.SemaphoreType.REGULAR, pltpu.SemaphoreType.REGULAR,
        ],
        compiler_params=pltpu.CompilerParams(
            collective_id=0, has_side_effects=True, vmem_limit_bytes=60 << 20
        ),
    )(queries, keys, values, chunk_decay, gain.reshape(1, 2 * WIDTH))


def solution(mesh):
    return jax.shard_map(
        local,
        mesh=mesh,
        in_specs=(
            P(("seq", "grp"), None), P(("seq", "grp"), None), P(("seq", "grp"), None),
            P("grp", "seq"), P("grp"),
        ),
        out_specs=P("seq", "grp"),
        check_vma=False,
    )
```

time: 79.8 us -> 78.8 us (0.987)
  the two profiles are of different devices: /device:TPU:1 before, /device:TPU:16 now
where the time goes in v3:
time: 78.8 us; the launch traced here: 78.7 us
  Pallas kernels  76.4 us (97%)
  local copies, waits for them, and re-layouts  2.26 us (3%)
    pallas_call x1, Pallas kernels, local(): pl.pallas_call(kernel, out_shape=jax.ShapeDtypeStruct((GROUP * ROWS, 2 *...  76.4 us
    unnamed x1, local copies, waits for them, and re-layouts  2.26 us

profile of v3, /device:TPU:16, one launch (start us, length us, event | category | flops | bytes accessed | tf_op | source)
XLA Modules:
  0.0 78.7 jit_solution(12195768053367897261)
XLA Ops:
  0.0 76.4 %shard_map.55 = bf16[2048,256]{1,0:T(8,128)(2,1)} custom-call(bf16[128,4096]{1,0:T(8,128)(2,1)} %q_hbm.1, bf16[128,4096]{1,0:T(8,128)(2,1)} %k_hbm.1, bf16[128,4096]{1,0:T(8,128)(2,1)} %v_hbm.1, f32[32,128]{1,0:T(8,128)} %bitcast.6, f32[1,256]{1,0:T(1,128)} %bitcast.7), custom_call_target="tpu_custom_call" | custom-call | tf_op jit(solution)/shard_map/pallas_call | solution.py:553
  76.4 2.3 %copy.8 = bf16[2048,256]{1,0:T(8,128)(2,1)} copy(bf16[2048,256]{1,0:T(8,128)(2,1)} %shard_map.55) | data formatting | bytes 2097152

commit v4 on v3

--- a/solution.py
+++ b/solution.py
@@ -13,6 +13,7 @@
 ROWS = 128
 WIDTH = 128
 X_SIZE = 4
+SHARE = WIDTH // X_SIZE
 Y_SIZE = 8
 KEPT, SENT = 1, 0
 
@@ -29,9 +30,10 @@
     q_own, k_own, v_own, level, total, level_out, level_in,
     q_in, state_own, state_sib, state_out, state_in, local_out, local_in, local_kept,
     block_out, x_state, x_total, row_out, y_state, y_total, tot_out, rowtot_out,
+    cross_out, cross_in,
     prefix, entering, carried, result, result_kept,
     load_sem, level_s, level_r, q_s, q_r, sib_s, sib_r, state_s, state_r, local_s, local_r,
-    x_s, x_r, xt_s, xt_r, y_s, y_r, yt_s, yt_r, enter_s, enter_r, pass_s, done_s, done_r,
+    x_s, x_r, xt_s, xt_r, y_s, y_r, yt_s, yt_r, cross_s, cross_r, enter_s, enter_r, pass_s, done_s, done_r,
     out_sem, hand_s, gate, sib_gate,
 ):
     g = lax.axis_index("grp")
@@ -128,9 +130,21 @@
             device_id=(p, s), device_id_type=MESH,
         )
 
+    def share(n):
+        return pl.ds(pl.multiple_of(n * SHARE, SHARE), SHARE)
+
+    def cross_copy(h, d, slot):
+        return pltpu.make_async_remote_copy(
+            src_ref=cross_out.at[h, lax.rem(x + d + 1, X_SIZE)],
+            dst_ref=cross_in.at[h, slot],
+            send_sem=cross_s.at[h, d], recv_sem=cross_r.at[h, slot],
+            device_id=(g, row_mates[d]), device_id_type=MESH,
+        )
+
     def x_copy(h, d, slot):
         return pltpu.make_async_remote_copy(
-            src_ref=block_out.at[h], dst_ref=x_state.at[h, slot],
+            src_ref=block_out.at[h, share(lax.rem(x + d + 1, X_SIZE)), :],
+            dst_ref=x_state.at[h, slot],
             send_sem=x_s.at[h, d], recv_sem=x_r.at[h, slot],
             device_id=(g, row_mates[d]), device_id_type=MESH,
         )
@@ -353,7 +367,7 @@
         block_out[h] = run.astype(BF16)
         for d in range(X_SIZE - 1):
             x_copy(h, d, x).start()
-        x_state[h, x] = block_out[h]
+        x_state[h, x] = block_out[h, share(x), :]
 
     def send_row(h):
         for d in range(1, X_SIZE):
@@ -366,20 +380,26 @@
             y_copy(h, d, y).start()
         y_state[h, y] = row_out[h]
 
-    def enter(h):
+    def cross(h):
         for d in range(Y_SIZE - 1):
             y_copy(h, d, lax.rem(y + d + 1, Y_SIZE)).wait_recv()
-        run = jnp.zeros((WIDTH, WIDTH), F32)
+        run = jnp.zeros((SHARE, WIDTH), F32)
         for n in range(Y_SIZE - 1):
             used = (n < y).astype(F32)
             run = jnp.exp(y_total[n, 4 * h : 4 * h + 1, :] * used) * run + (
                 y_state[h, n].astype(F32) * used
             )
-        for n in range(X_SIZE - 1):
-            used = (n < x).astype(F32)
-            run = jnp.exp(x_total[n, 4 * h : 4 * h + 1, :] * used) * run + (
-                x_state[h, n].astype(F32) * used
-            )
+        for n in range(X_SIZE):
+            cross_out[h, n] = run
+            run = jnp.exp(x_total[n, 4 * h : 4 * h + 1, :]) * run + x_state[h, n].astype(F32)
+        for d in range(X_SIZE - 1):
+            cross_copy(h, d, x).start()
+        cross_in[h, x] = cross_out[h, x]
+
+    def enter(h):
+        for d in range(1, X_SIZE):
+            cross_copy(h, d - 1, lax.rem(x + d, X_SIZE)).wait_recv()
+        run = cross_in[h].reshape(WIDTH, WIDTH)
         for n in range(CHIPS):
             prefix[h, n] = run.astype(BF16)
             run = chip_share(n, h) * run + state_in[h, n].astype(F32)
@@ -400,6 +420,7 @@
         yt_copy(d, lax.rem(y + d + 1, Y_SIZE)).wait_recv()
     send_row(KEPT)
     send_block(SENT)
+    cross(KEPT)
     enter(KEPT)
 
     @pl.loop(0, CHIPS - 1)
@@ -435,6 +456,8 @@
         finish_kept(p)
         done_copy(p, g).start()
 
+    cross(SENT)
+
     @pl.loop(0, CHIPS)
     def _(i):
         p = lax.rem(z + 2 * CHIPS - order(2 * i)[0], CHIPS) * 2 + 1 - c
@@ -509,6 +532,7 @@
 
         for d in range(X_SIZE - 1):
             x_copy(h, d, x).wait_send()
+            cross_copy(h, d, x).wait_send()
         for d in range(Y_SIZE - 1):
             y_copy(h, d, y).wait_send()
 
@@ -567,11 +591,12 @@
             wide_parts(GROUP, 2), wide_parts(GROUP, 2),
             parts(2, CHIPS), parts(2, CHIPS),
             parts(GROUP), parts(GROUP), wide_parts(GROUP),
-            parts(2), parts(2, X_SIZE),
+            parts(2), pltpu.VMEM((2, X_SIZE, SHARE, WIDTH), BF16),
             pltpu.VMEM((X_SIZE, 8, ROWS), F32),
-            parts(2), parts(2, Y_SIZE),
+            pltpu.VMEM((2, SHARE, WIDTH), BF16), pltpu.VMEM((2, Y_SIZE, SHARE, WIDTH), BF16),
             pltpu.VMEM((Y_SIZE, 8, ROWS), F32),
             tile, tile,
+            pltpu.VMEM((2, X_SIZE, SHARE, WIDTH), F32), pltpu.VMEM((2, X_SIZE, SHARE, WIDTH), F32),
             parts(2, CHIPS), parts(GROUP), wide_parts(GROUP), parts(GROUP), parts(GROUP),
             dma((6,)),
             dma((GROUP,)), dma((GROUP,)),
@@ -581,6 +606,7 @@
             dma((GROUP,)), dma((GROUP,)),
             dma((2, X_SIZE)), dma((2, X_SIZE)), dma((X_SIZE,)), dma((X_SIZE,)),
             dma((2, Y_SIZE)), dma((2, Y_SIZE)), dma((Y_SIZE,)), dma((Y_SIZE,)),
+            dma((2, X_SIZE)), dma((2, X_SIZE)),
             dma((CHIPS,)), dma((GROUP,)), dma((GROUP,)), dma((GROUP,)), dma((GROUP,)),
             dma((GROUP,)), dma((GROUP,)),
             pltpu.SemaphoreType.REGULAR, pltpu.SemaphoreType.REGULAR,

time: 78.8 us -> 77.9 us (0.989)
  the two profiles are of different devices: /device:TPU:16 before, /device:TPU:1 now
where the time goes in v4:
time: 77.9 us; the launch traced here: 77.7 us
  Pallas kernels  75.4 us (97%)
  local copies, waits for them, and re-layouts  2.26 us (3%)
    pallas_call x1, Pallas kernels, local(): pl.pallas_call(kernel, out_shape=jax.ShapeDtypeStruct((GROUP * ROWS, 2 *...  75.4 us
    unnamed x1, local copies, waits for them, and re-layouts  2.26 us

profile of v4, /device:TPU:1, one launch (start us, length us, event | category | flops | bytes accessed | tf_op | source)
XLA Modules:
  0.0 77.7 jit_solution(881646547769484708)
XLA Ops:
  0.0 75.4 %shard_map.55 = bf16[2048,256]{1,0:T(8,128)(2,1)} custom-call(bf16[128,4096]{1,0:T(8,128)(2,1)} %q_hbm.1, bf16[128,4096]{1,0:T(8,128)(2,1)} %k_hbm.1, bf16[128,4096]{1,0:T(8,128)(2,1)} %v_hbm.1, f32[32,128]{1,0:T(8,128)} %bitcast.6, f32[1,256]{1,0:T(1,128)} %bitcast.7), custom_call_target="tpu_custom_call" | custom-call | tf_op jit(solution)/shard_map/pallas_call | solution.py:577
  75.4 2.3 %copy.8 = bf16[2048,256]{1,0:T(8,128)(2,1)} copy(bf16[2048,256]{1,0:T(8,128)(2,1)} %shard_map.55) | data formatting | bytes 2097152
